TPU v7x, 1024 devices: a whole 4x4x32 slice. The times are simulated.
1024 devices in a mesh: row: 32 (over z), col: 16 (over y, x), layer: 2 (over core).
Axes of the slice: x: 4, y: 4, z: 32, core: 2. Of those that a mesh axis runs over, the one named last changes fastest.
Arguments:
- left_blocks: bfloat16 [8192, 2, 4096], P('row', 'layer', 'col'), may hold values from 4.8577785e-06 to 0.00048828125
- batch_blocks: bfloat16 [2, 4096, 8192], P('layer', 'row', 'col'), may hold values from 0.019897461 to 2
- left_mask: int32 [64, 2, 32], P('row', 'layer', 'col'), may hold values 0 or 1
- batch_mask: int32 [2, 32, 64], P('layer', 'row', 'col'), may hold values 0 or 1
- prune_mask: int32 [64, 64], P('row', ('col', 'layer')), may hold values 0 or 1
Outputs:
- normalized: float32 [8192, 8192], P('row', ('col', 'layer'))
All inputs are finite; a program needn't handle non-finite values. No bound on the sum of `left_mask` or of `batch_mask` or of `prune_mask` on one device may be relied on, other than what follows from the above.
Results may differ from a plain program's by a relative error of at most 0.0003.
Values may be sent and summed in bfloat16 or wider, within the bound.
A program may use at most 32 MiB of HBM per device.

v0:
```python
import jax
import jax.numpy as jnp
from jax import lax
from jax.sharding import PartitionSpec as P

epsilon = 1e-06


def widen_left(mask, tile_size):
    first, middle, last = mask.shape
    spread = jnp.broadcast_to(
        mask.astype(jnp.bfloat16)[:, None, :, :, None], (first, tile_size, middle, last, tile_size)
    )
    return spread.reshape(first * tile_size, middle, last * tile_size)


def widen_right(mask, tile_size):
    first, middle, last = mask.shape
    spread = jnp.broadcast_to(
        mask.astype(jnp.bfloat16)[:, :, None, :, None], (first, middle, tile_size, last, tile_size)
    )
    return spread.reshape(first, middle * tile_size, last * tile_size)


def widen_pair(mask, tile_size):
    first, last = mask.shape
    spread = jnp.broadcast_to(
        mask.astype(jnp.float32)[:, None, :, None], (first, tile_size, last, tile_size)
    )
    return spread.reshape(first * tile_size, last * tile_size)


def on_device(left_blocks, batch_blocks, left_mask, batch_mask, prune_mask):
    tile_size = left_blocks.shape[0] // left_mask.shape[0]
    left = left_blocks * widen_left(left_mask, tile_size)
    right = batch_blocks * widen_right(batch_mask, tile_size)
    row_count = left.shape[0]
    complete_right = lax.all_gather(right, "row", axis=1, tiled=True)[0]
    product = jnp.dot(
        lax.all_gather(left, "col", axis=2, tiled=True)[:, 0, :],
        complete_right,
        preferred_element_type=jnp.float32,
    )
    own_share = lax.psum_scatter(product, "layer", scatter_dimension=1, tiled=True)
    inflated = own_share * own_share * widen_pair(prune_mask, tile_size)
    col_sums = lax.psum(jnp.sum(inflated, axis=0), "row")
    total_rows = row_count * lax.axis_size("row")
    return inflated * (total_rows / (col_sums + epsilon))


def solution(mesh):
    placed = (
        P("row", "layer", "col"),
        P("layer", "row", "col"),
        P("row", "layer", "col"),
        P("layer", "row", "col"),
        P("row", ("col", "layer")),
    )
    return jax.shard_map(
        on_device, mesh=mesh, in_specs=placed, out_specs=P("row", ("col", "layer")), check_vma=False
    )
```

profile of v0, /device:TPU:6, one launch (start us, length us, event | category | flops | bytes accessed | tf_op | source)
XLA Modules:
  0.0 341.0 jit_solution(898186911816580992)
XLA Ops:
  6.5 0.0 all-gather.3.cloned.1.call-start
  6.5 0.7 convert_element_type.9
  7.2 0.1 broadcast_in_dim.30
  7.4 0.1 broadcast_in_dim.31
  7.5 1.6 mul.20
  9.1 0.0 all-gather.3.cloned.1.call-update
  9.1 0.0 all-gather.5.cloned.1.call-start
  9.1 0.7 convert_bitcast_fusion
  9.8 0.1 broadcast_bitcast_fusion
  9.9 1.6 broadcast_multiply_fusion.1
  11.4 0.0 copy-start
  11.4 0.0 all-gather.5.cloned.1.call-update
  11.5 0.0 reduce-scatter.2.cloned.1.call-start
  11.5 90.7 %all-gather.3.cloned.1.call-done = bf16[256,1,4096]{2,0,1:T(8,128)(2,1)} async-done(((bf16[256,1,256]{2,0,1:T(8,128)(2,1)}), bf16[256,1,4096]{2,0,1:T(8,128)(2,1)}) %all-gather.3.cloned.1.call-update) | async-done | bytes 2097168 | tf_op jit(solution)/shard_map/all_gather | solution.py:40
  102.2 146.5 %all-gather.5.cloned.1.call-done = bf16[1,4096,512]{2,1,0:T(8,128)(2,1)} async-done(((bf16[1,128,512]{2,1,0:T(8,128)(2,1)}), bf16[1,4096,512]{2,1,0:T(8,128)(2,1)}) %all-gather.5.cloned.1.call-update) | async-done | bytes 4194320 | tf_op jit(solution)/shard_map/all_gather | solution.py:38
  248.7 4.9 %fusion = f32[256,512]{1,0:T(8,128)} fusion(bf16[1,4096,512]{2,1,0:T(8,128)(2,1)} %all-gather.5.cloned.1.call-done, bf16[256,1,4096]{2,0,1:T(8,128)(2,1)} %all-gather.3.cloned.1.call-done), kind=kOutput, calls=%fused_computation | convolution fusion | flops 1073741824 | bytes 6815744 | tf_op jit(solution)/shard_map/dot_general | solution.py:39
  253.5 0.0 reduce-scatter.2.cloned.1.call-update
  253.6 0.0 copy-done
  253.6 19.2 %reduce-scatter.2.cloned.1.call-done = f32[256,256]{1,0:T(8,128)} async-done(((f32[256,512]{1,0:T(8,128)}), f32[256,256]{1,0:T(8,128)}) %reduce-scatter.2.cloned.1.call-update) | async-done | bytes 262160 | tf_op jit(solution)/shard_map/reduce_scatter | solution.py:44
  272.7 0.1 broadcast_in_dim.36
  272.9 1.0 fusion.3
  273.9 58.9 %psum.7 = f32[256]{0:T(256)S(1)} all-reduce(f32[256]{0:T(256)S(1)} %fusion.3), channel_id=1, replica_groups=mesh['row'=32,'col'=16,'layer'=2] {'row'}, use_global_device_ids=true, to_apply=%region_2.0 | all-reduce | flops 256 | bytes 2048 | tf_op jit(solution)/shard_map/psum | solution.py:46
  332.8 1.7 broadcast_multiply_fusion
  (3 shorter events, 0.0 us)
Async XLA Ops:
  6.5 95.7 %all-gather.3.cloned.1.call-start = ((), (), s32[]{:S(2)}) async-start(), calls=%async_computation.1 | async-start | bytes 2228224 | tf_op jit(solution)/shard_map/all_gather | solution.py:40
  9.1 239.6 %all-gather.5.cloned.1.call-start = ((), (), s32[]{:S(2)}) async-start(), calls=%async_computation.2 | async-start | bytes 4325376 | tf_op jit(solution)/shard_map/all_gather | solution.py:38
  11.4 242.1 %copy-start = (s32[2,2]{1,0:T(2,128)S(1)}, s32[2,2]{1,0:T(2,128)}, u32[]{:S(2)}) copy-start(s32[2,2]{1,0:T(2,128)} %param.9) | copy-start | bytes 52
  11.5 261.3 %reduce-scatter.2.cloned.1.call-start = ((), (), s32[]{:S(2)}) async-start(), calls=%async_computation.3 | async-start | bytes 786432 | tf_op jit(solution)/shard_map/reduce_scatter | solution.py:44
Sparse Core Ops, SparseCore 0:
  11.5 90.6 all-gather.2
  104.9 143.7 all-gather.4
  253.7 19.0 reduce-scatter.1
where the time goes:
time: 341 us
  waiting for transfers between devices  256 us (75%)
  blocking collectives  58.9 us (17%)
  between operations  13.1 us (4%)
  other arithmetic  7.21 us (2%)
  matrix products  4.87 us (1%)
    all_gather x1, waiting for transfers between devices, on_device(): complete_right = lax.all_gather(right, 'row', axis=1, tiled=True)[0]  146 us
    all_gather x1, waiting for transfers between devices, on_device(): lax.all_gather(left, 'col', axis=2, tiled=True)[:, 0, :]  90.7 us
    psum x1, blocking collectives, on_device(): col_sums = lax.psum(jnp.sum(inflated, axis=0), 'row')  58.9 us
    reduce_scatter x1, waiting for transfers between devices, on_device(): lax.psum_scatter(product, 'layer', scatter_dimension=1, tiled=True)  19.2 us
  transfers between devices with their start and end apart: 3, of which 3 were waited for; matrix products, arithmetic and copies ran while one was open for 1% of the time, Pallas kernels for 0%

commit v1 on v0

v1 whole, which is shorter than its diff:
```python
import functools

import jax
import jax.numpy as jnp
from jax import lax
from jax.experimental import pallas as pl
from jax.experimental.pallas import tpu as pltpu
from jax.sharding import PartitionSpec as P

epsilon = 1e-06
MESH = pl.DeviceIdType.MESH
SIDE = 4


def kernel(
    nz,
    left_ref,
    right_ref,
    left_mask,
    right_mask,
    prune_mask,
    out_ref,
    left_in,
    right_in,
    left_all,
    right_all,
    right_swap,
    acc,
    own_sum,
    near_sums,
    window_sum,
    far_sums,
    in_sem,
    swap_sem,
    ring_send,
    ring_recv,
    first_send,
    first_recv,
    second_send,
    second_recv,
    pass_sem,
    near_send,
    near_recv,
    far_send,
    far_recv,
):
    r = lax.axis_index("row")
    c = lax.axis_index("col")
    l = lax.axis_index("layer")
    other = 1 - l
    y, x = c // SIDE, c % SIDE

    def at_z(step):
        return (lax.rem(r + step + nz, nz), c, l)

    def at_x(step):
        return (r, y * SIDE + lax.rem(x + step, SIDE), l)

    def at_y(step):
        return (r, lax.rem(y + step, SIDE) * SIDE + x, l)

    partner = (r, c, other)

    take_left = pltpu.make_async_copy(left_ref, left_in, in_sem.at[0])
    take_right = pltpu.make_async_copy(right_ref, right_in, in_sem.at[1])
    take_right.start()
    take_left.start()

    barrier = pltpu.get_barrier_semaphore()
    greeted = [at_z(1), at_z(-1), partner]
    for step in range(1, SIDE):
        greeted += [at_x(step), at_y(step)]
    for device in greeted:
        pl.semaphore_signal(barrier, inc=1, device_id=device, device_id_type=MESH)

    tile = left_in.shape[1] // 2
    half = right_in.shape[1] // 2
    take_right.wait()
    for part in range(half // tile):
        mask = right_mask[0, 0, 2 * l + part].astype(jnp.float32)
        block = right_in[:, pl.ds(pl.multiple_of(l * half + part * tile, tile), tile)]
        right_all[l, r, :, part * tile : (part + 1) * tile] = (block.astype(jnp.float32) * mask).astype(jnp.bfloat16)
        mask = right_mask[0, 0, 2 * other + part].astype(jnp.float32)
        block = right_in[:, pl.ds(pl.multiple_of(other * half + part * tile, tile), tile)]
        right_swap[:, part * tile : (part + 1) * tile] = (block.astype(jnp.float32) * mask).astype(jnp.bfloat16)
    take_left.wait()
    for tall in range(2):
        for wide in range(2):
            mask = left_mask[tall, 0, wide].astype(jnp.float32)
            block = left_in[tall * tile : (tall + 1) * tile, wide * tile : (wide + 1) * tile]
            left_all[l, 2 * c + wide, tall * tile : (tall + 1) * tile, :] = (block.astype(jnp.float32) * mask).astype(
                jnp.bfloat16
            )
    acc[...] = jnp.zeros_like(acc)
    pl.semaphore_wait(barrier, len(greeted))

    hops = ((nz // 2, nz // 2 - 1), (nz // 2 - 1, nz // 2))
    slices = (l, other)
    ways = (1, -1)

    def origin(way, step):
        return lax.rem(r - ways[way] * (step + 1) + 2 * nz, nz)

    def ring_copy(way, kind, step):
        block = right_all.at[slices[kind], origin(way, step - 1)]
        return pltpu.make_async_remote_copy(
            src_ref=block,
            dst_ref=block,
            send_sem=ring_send.at[way, kind, step],
            recv_sem=ring_recv.at[way, kind, step],
            device_id=at_z(ways[way]),
            device_id_type=MESH,
        )

    def ring_arrived(way, kind, step):
        block = right_all.at[slices[kind], origin(way, step)]
        pltpu.make_async_remote_copy(
            src_ref=block,
            dst_ref=block,
            send_sem=ring_send.at[way, kind, step],
            recv_sem=ring_recv.at[way, kind, step],
            device_id=at_z(ways[way]),
            device_id_type=MESH,
        ).wait_recv()

    swap = pltpu.make_async_remote_copy(
        src_ref=right_swap,
        dst_ref=right_all.at[l, r],
        send_sem=swap_sem.at[0],
        recv_sem=swap_sem.at[1],
        device_id=partner,
        device_id_type=MESH,
    )
    swap.start()
    for way in range(2):
        ring_copy(way, 0, 0).start()

    peers = (at_x, at_y)

    def piece(way, back):
        if way == 0:
            return 2 * (y * SIDE + lax.rem(x + SIDE - back, SIDE))
        return 2 * (lax.rem(y + SIDE - back, SIDE) * SIDE + x) + 1

    def first_copy(way, step, place):
        block = left_all.at[l, place]
        return pltpu.make_async_remote_copy(
            src_ref=block,
            dst_ref=block,
            send_sem=first_send.at[way, step - 1],
            recv_sem=first_recv.at[way, step - 1],
            device_id=peers[way](step),
            device_id_type=MESH,
        )

    def second_copy(way, back, step, place):
        block = left_all.at[l, place]
        return pltpu.make_async_remote_copy(
            src_ref=block,
            dst_ref=block,
            send_sem=second_send.at[way, back, step - 1],
            recv_sem=second_recv.at[way, back, step - 1],
            device_id=peers[1 - way](step),
            device_id_type=MESH,
        )

    def far_place(way, back, step):
        if way == 0:
            return 2 * (lax.rem(y + SIDE - step, SIDE) * SIDE + lax.rem(x + SIDE - back, SIDE))
        return 2 * (lax.rem(y + SIDE - back, SIDE) * SIDE + lax.rem(x + SIDE - step, SIDE)) + 1

    for step in range(1, SIDE):
        for way in range(2):
            first_copy(way, step, piece(way, 0)).start()
    for step in range(1, SIDE):
        for way in range(2):
            second_copy(way, 0, step, piece(way, 0)).start()

    swap.wait_recv()
    for way in range(2):
        ring_copy(way, 1, 0).start()

    def ring_step(step, last=0):
        for kind in range(2):
            for way in range(2):
                if last and step >= hops[way][kind]:
                    continue
                ring_arrived(way, kind, step)
                if not last or step + 1 < hops[way][kind]:
                    ring_copy(way, kind, step + 1).start()

    def multiply(kind, row):
        acc[...] += jnp.dot(
            left_all[slices[kind], row], right_all[slices[kind], row], preferred_element_type=jnp.float32
        )

    def multiply_step(step):
        for way in range(2):
            for kind in range(2):
                multiply(kind, origin(way, step))

    ring_step(0)
    ring_step(1)
    for back in range(1, SIDE):
        for way in range(2):
            first_copy(way, back, piece(way, back)).wait_recv()
            for step in range(1, SIDE):
                second_copy(way, back, step, piece(way, back)).start()
    middle = nz // 4
    lax.fori_loop(2, middle, lambda step, _: (ring_step(step), None)[1], None)
    for step in range(1, SIDE):
        for back in range(SIDE):
            for way in range(2):
                second_copy(way, back, step, far_place(way, back, step)).wait_recv()
    hand_over = pltpu.make_async_remote_copy(
        src_ref=left_all.at[l],
        dst_ref=left_all.at[l],
        send_sem=pass_sem.at[0],
        recv_sem=pass_sem.at[1],
        device_id=partner,
        device_id_type=MESH,
    )
    hand_over.start()
    ring_step(middle)
    ring_step(middle + 1)
    pltpu.make_async_remote_copy(
        src_ref=left_all.at[other],
        dst_ref=left_all.at[other],
        send_sem=pass_sem.at[0],
        recv_sem=pass_sem.at[1],
        device_id=partner,
        device_id_type=MESH,
    ).wait_recv()
    for kind in range(2):
        multiply(kind, r)
    begin = middle + 2
    end = nz // 2 - 2
    each = begin // (end - begin) + 1

    def both(step, _):
        ring_step(step)
        for turn in range(each):
            multiply_step(each * (step - begin) + turn)

    lax.fori_loop(begin, end, both, None)
    done = each * (end - begin)
    ring_step(end, last=1)
    for step in range(done, end + 1):
        multiply_step(step)
    ring_step(end + 1, last=1)
    multiply(0, origin(0, end + 1))
    multiply(1, origin(1, end + 1))

    rows, columns = acc.shape
    for tall in range(2):
        for wide in range(2):
            span = (slice(tall * tile, (tall + 1) * tile), slice(wide * tile, (wide + 1) * tile))
            value = acc[span]
            acc[span] = value * value * prune_mask[tall, wide].astype(jnp.float32)
    own_sum[0] = jnp.sum(acc[...], axis=0, keepdims=True)

    window = nz // 4
    near = [step for step in range(-(window // 2 - 1), window // 2 + 1) if step]

    def near_copy(index, step):
        return pltpu.make_async_remote_copy(
            src_ref=own_sum.at[0],
            dst_ref=near_sums.at[index],
            send_sem=near_send.at[index],
            recv_sem=near_recv.at[index],
            device_id=at_z(step),
            device_id_type=MESH,
        )

    for index, step in sorted(enumerate(near), key=lambda pair: -abs(pair[1])):
        near_copy(index, step).start()
    total = own_sum[0]
    for index, step in enumerate(near):
        near_copy(index, step).wait_recv()
    for index in range(len(near)):
        total += near_sums[index]
    window_sum[0] = total
    far = (window // 2, -(window // 2), window // 2 + window, -(window // 2 + window))

    def far_copy(index, step):
        return pltpu.make_async_remote_copy(
            src_ref=window_sum.at[0],
            dst_ref=far_sums.at[index],
            send_sem=far_send.at[index],
            recv_sem=far_recv.at[index],
            device_id=at_z(step),
            device_id_type=MESH,
        )

    for index, step in reversed(list(enumerate(far))):
        far_copy(index, step).start()

    swap.wait_send()
    hand_over.wait_send()
    for way in range(2):
        for step in range(1, SIDE):
            first_copy(way, step, piece(way, 0)).wait_send()
            for back in range(SIDE):
                second_copy(way, back, step, piece(way, back)).wait_send()

    def ring_left(step, _):
        for way in range(2):
            for kind in range(2):
                ring_copy(way, kind, step).wait_send()

    lax.fori_loop(0, nz // 2 - 1, ring_left, None)
    ring_copy(0, 0, nz // 2 - 1).wait_send()
    ring_copy(1, 1, nz // 2 - 1).wait_send()
    for index, step in enumerate(near):
        near_copy(index, step).wait_send()

    for index, step in enumerate(far):
        far_copy(index, step).wait_recv()
    total = far_sums[0]
    for index in range(1, len(far)):
        total += far_sums[index]
    out_ref[...] = acc[...] * ((rows * nz) / (total + epsilon))
    for index, step in enumerate(far):
        far_copy(index, step).wait_send()


def on_device(nz, left_blocks, batch_blocks, left_mask, batch_mask, prune_mask):
    rows, _, depth = left_blocks.shape
    _, inner, columns = batch_blocks.shape
    tile = rows // left_mask.shape[0]
    half = columns // 2
    left = left_blocks.reshape(rows, depth)
    right = batch_blocks.reshape(inner, columns)
    dma = pltpu.SemaphoreType.DMA
    hbm = pl.BlockSpec(memory_space=pl.ANY)
    smem = pl.BlockSpec(memory_space=pltpu.SMEM)
    window = nz // 4
    return pl.pallas_call(
        functools.partial(kernel, nz),
        out_shape=jax.ShapeDtypeStruct((rows, half), jnp.float32),
        in_specs=[hbm, hbm, smem, smem, smem],
        out_specs=pl.BlockSpec(memory_space=pltpu.VMEM),
        scratch_shapes=[
            pltpu.VMEM((rows, depth), jnp.bfloat16),
            pltpu.VMEM((inner, columns), jnp.bfloat16),
            pltpu.VMEM((2, 2 * SIDE * SIDE, rows, tile), jnp.bfloat16),
            pltpu.VMEM((2, nz, inner, half), jnp.bfloat16),
            pltpu.VMEM((inner, half), jnp.bfloat16),
            pltpu.VMEM((rows, half), jnp.float32),
            pltpu.VMEM((1, 1, half), jnp.float32),
            pltpu.VMEM((window - 1, 1, half), jnp.float32),
            pltpu.VMEM((1, 1, half), jnp.float32),
            pltpu.VMEM((4, 1, half), jnp.float32),
            dma((2,)),
            dma((2,)),
            dma((2, 2, nz // 2)),
            dma((2, 2, nz // 2)),
            dma((2, SIDE - 1)),
            dma((2, SIDE - 1)),
            dma((2, SIDE, SIDE - 1)),
            dma((2, SIDE, SIDE - 1)),
            dma((2,)),
            dma((window - 1,)),
            dma((window - 1,)),
            dma((4,)),
            dma((4,)),
        ],
        compiler_params=pltpu.CompilerParams(collective_id=0, has_side_effects=True),
    )(left, right, left_mask, batch_mask, prune_mask)


def solution(mesh):
    placed = (
        P("row", "layer", "col"),
        P("layer", "row", "col"),
        P("row", "layer", "col"),
        P("layer", "row", "col"),
        P("row", ("col", "layer")),
    )
    return jax.shard_map(
        functools.partial(on_device, mesh.shape["row"]),
        mesh=mesh,
        in_specs=placed,
        out_specs=P("row", ("col", "layer")),
        check_vma=False,
    )
```

time: 341 us -> 102 us (0.30)
  waiting for transfers between devices: 256 us -> 0 us
  Pallas kernels: 0 us -> 100 us
  blocking collectives: 58.9 us -> 0 us
  between operations: 13.1 us -> 0.01 us
  other arithmetic: 7.21 us -> 0 us
  matrix products: 4.87 us -> 0 us
    all_gather x2 -> x0, waiting for transfers between devices: 237 us -> none  [the longest x1 146 us: on_device(): complete_right = lax.all_gather(right, 'row', axis=1, tiled=True)[0]]
    pallas_call x0 -> x1, Pallas kernels: none -> 100 us  [on_device(): pl.pallas_call(functools.partial(kernel, nz), out_shape=jax.ShapeDtypeStr...]
    psum x1 -> x0, blocking collectives: 58.9 us -> none  [on_device(): col_sums = lax.psum(jnp.sum(inflated, axis=0), 'row')]
    reduce_scatter x1 -> x0, waiting for transfers between devices: 19.2 us -> none  [on_device(): lax.psum_scatter(product, 'layer', scatter_dimension=1, tiled=True)]
    dot_general x1 -> x0, matrix products: 4.87 us -> none  [on_device(): jnp.dot(lax.all_gather(left, 'col', axis=2, tiled=True)[:, 0, :], complet...]
    mul x3 -> x0, other arithmetic: 4.85 us -> none  [the longest x1 1.69 us: on_device(): return inflated * (total_rows / (col_sums + epsilon))]
  transfers between devices with their start and end apart: 3 -> 0, of which waited for: 3 -> 0; matrix products, arithmetic and copies ran while one was open for 1% -> 0% of each run, Pallas kernels for 0% -> 0%
where the time goes in v1:
time: 102 us
  Pallas kernels  100 us (98%)
  local copies, waits for them, and re-layouts  1.67 us (2%)
    pallas_call x1, Pallas kernels, on_device(): pl.pallas_call(functools.partial(kernel, nz), out_shape=jax.ShapeDtypeStr...  100 us

profile of v1, /device:TPU:6, one launch (start us, length us, event | category | flops | bytes accessed | tf_op | source)
XLA Modules:
  0.0 101.8 jit_solution(14690844841947969470)
XLA Ops:
  0.0 100.1 %shard_map.55 = f32[256,256]{1,0:T(8,128)} custom-call(bf16[256,256]{1,0:T(8,128)(2,1)} %bitcast.2, bf16[128,512]{1,0:T(8,128)(2,1)} %bitcast.3, s32[2,1,2]{2,1,0:T(1,128)} %left_mask.1, s32[1,1,4]{2,1,0:T(1,128)} %right_mask.1, s32[2,2]{1,0:T(2,128)} %prune_mask.1), custom_call_target="tpu_custom_call" | custom-call | tf_op jit(solution)/shard_map/pallas_call | solution.py:338
  100.1 1.7 %copy.7 = f32[256,256]{1,0:T(8,128)} copy(f32[256,256]{1,0:T(8,128)} %shard_map.55) | data formatting | bytes 524288

commit v2 on v0

v2 whole, which is shorter than its diff:
```python
import functools

import jax
import jax.numpy as jnp
from jax import lax
from jax.experimental import pallas as pl
from jax.experimental.pallas import tpu as pltpu
from jax.sharding import PartitionSpec as P

epsilon = 1e-06
MESH = pl.DeviceIdType.MESH
SIDE = 4


def kernel(
    nz,
    left_ref,
    right_ref,
    left_mask,
    right_mask,
    prune_mask,
    out_ref,
    left_in,
    right_in,
    left_all,
    right_all,
    acc,
    own_sum,
    sums,
    in_sem,
    swap_send,
    swap_recv,
    ring_send,
    ring_recv,
    pass_send,
    pass_recv,
    left_send,
    first_recv,
    second_recv,
    left_pass_send,
    left_pass_recv,
    sum_sem,
):
    r = lax.axis_index("row")
    c = lax.axis_index("col")
    l = lax.axis_index("layer")
    y, x = c // SIDE, c % SIDE
    deep = left_all.shape[3]
    tile = deep
    half = right_all.shape[3]
    slots = ring_recv.shape[2]

    def at_z(step):
        return (lax.rem(r + step + nz, nz), c, l)

    def at_x(step):
        return (r, y * SIDE + lax.rem(x + step, SIDE), l)

    def at_y(step):
        return (r, lax.rem(y + step, SIDE) * SIDE + x, l)

    partner = (r, c, 1 - l)

    def send(block, send_sem, recv_sem, device):
        return pltpu.make_async_remote_copy(
            src_ref=block,
            dst_ref=block,
            send_sem=send_sem,
            recv_sem=recv_sem,
            device_id=device,
            device_id_type=MESH,
        )

    take_right = pltpu.make_async_copy(right_ref, right_in, in_sem.at[0])
    take_left = pltpu.make_async_copy(left_ref, left_in, in_sem.at[1])
    take_right.start()
    take_left.start()

    barrier = pltpu.get_barrier_semaphore()

    def greet(devices):
        for device in devices:
            pl.semaphore_signal(barrier, inc=1, device_id=device, device_id_type=MESH)

    greet([partner])
    ring_greeted = [at_z(1), at_z(-1)]
    left_greeted = [peer(step) for step in range(1, SIDE) for peer in (at_x, at_y)]
    pl.when(l == 1)(lambda: greet(ring_greeted))
    pl.when(l == 0)(lambda: greet(left_greeted))

    own_slice = pl.ds(pl.multiple_of(l * deep, deep), deep)
    take_right.wait()
    for h in range(2):
        for part in range(half // tile):
            mask = right_mask[0, 0, h * (half // tile) + part].astype(jnp.float32)
            block = right_in[:, h * half + part * tile : h * half + (part + 1) * tile]
            right_all[r, h, own_slice, part * tile : (part + 1) * tile] = (block.astype(jnp.float32) * mask).astype(
                jnp.bfloat16
            )
    take_left.wait()
    for tall in range(2):
        for wide in range(2):
            mask = left_mask[tall, 0, wide].astype(jnp.float32)
            block = left_in[tall * tile : (tall + 1) * tile, wide * tile : (wide + 1) * tile]
            left_all[2 * c + wide, l, tall * tile : (tall + 1) * tile, :] = (block.astype(jnp.float32) * mask).astype(
                jnp.bfloat16
            )

    ways = (1, -1)

    def origin(way, step):
        return lax.rem(r - ways[way] * (step + 1) + 2 * nz, nz)

    def multiply(row, first=False):
        left = jnp.concatenate([left_all[row, 0], left_all[row, 1]], axis=1)
        product = jnp.dot(left, right_all[row, l], preferred_element_type=jnp.float32)
        acc[...] = product if first else acc[...] + product

    def multiply_step(step):
        for way in range(2):
            multiply(origin(way, step))

    right_swap_0 = send(right_all.at[r, :, pl.ds(0, deep)], swap_send.at[0], swap_recv.at[0], partner)
    right_swap_1 = send(right_all.at[r, 0, pl.ds(deep, deep)], swap_send.at[0], swap_recv.at[0], partner)
    left_swap_0 = send(left_all.at[pl.ds(2 * c, 2), 0], left_pass_send.at[0], left_pass_recv.at[0], partner)
    left_swap_1 = send(left_all.at[pl.ds(2 * c, 2), 1], swap_send.at[1], swap_recv.at[1], partner)
    steps = nz // 2

    def pass_group(step):
        if isinstance(step, int) and step >= steps - 2:
            return (steps - 2 + 3) // 4 + step - (steps - 2)
        return step // 4

    @pl.when(l == 1)
    def _():
        pl.semaphore_wait(barrier, 1 + len(ring_greeted))
        kinds = ((1, 0), (1, 1), (0, 0), (0, 1))
        hops = ((steps - 1, steps), (steps, steps - 1))

        def block(kind, row):
            s, h = kinds[kind]
            return right_all.at[row, h, pl.ds(s * deep, deep)]

        def ring_copy(way, kind, step, row):
            return send(
                block(kind, row), ring_send.at[0], ring_recv.at[way, kind, lax.rem(step, slots)], at_z(ways[way])
            )

        for kind in range(2):
            for way in range(2):
                ring_copy(way, kind, 0, r).start()
        right_swap_1.start()
        left_swap_1.start()
        right_swap_0.wait_recv()
        for kind in range(2, 4):
            for way in range(2):
                ring_copy(way, kind, 0, r).start()

        def ring_step(step, last=False):
            for kind, (s, h) in enumerate(kinds):
                for way in range(2):
                    if last and step >= hops[s][way]:
                        continue
                    row = origin(way, step)
                    ring_copy(way, kind, step, row).wait_recv()
                    if not last or step + 1 < hops[s][way]:
                        ring_copy(way, kind, step + 1, row).start()
                    if h == 0:
                        send(block(kind, row), pass_send.at[0], pass_recv.at[pass_group(step)], partner).start()

        begin = steps - 6
        end = steps - 2
        each = begin // (end - begin) + 1
        lax.fori_loop(0, begin, lambda step, _: (ring_step(step), None)[1], None)
        send(left_all.at[pl.ds(0, nz - 1)], left_pass_send.at[0], left_pass_recv.at[0], partner).wait_recv()
        multiply(r, first=True)

        def both(step, _):
            ring_step(step)
            for turn in range(each):
                multiply_step(each * (step - begin) + turn)

        lax.fori_loop(begin, end, both, None)
        ring_step(end, last=True)
        for step in range(each * (end - begin), end + 1):
            multiply_step(step)
        ring_step(end + 1, last=True)
        multiply(origin(0, end + 1))

    @pl.when(l == 0)
    def _():
        pl.semaphore_wait(barrier, 1 + len(left_greeted))
        right_swap_0.start()
        left_swap_0.start()
        left_swap_1.wait_recv()
        peers = (at_x, at_y)

        def place(way, back, step=0):
            to_x, to_y = (back, step) if way == 0 else (step, back)
            return 2 * (lax.rem(y + SIDE - to_y, SIDE) * SIDE + lax.rem(x + SIDE - to_x, SIDE)) + way

        def first_copy(way, step, chunk):
            return send(left_all.at[chunk], left_send.at[0], first_recv.at[way, step - 1], peers[way](step))

        def second_copy(way, back, step, chunk):
            return send(left_all.at[chunk], left_send.at[0], second_recv.at[way, back], peers[1 - way](step))

        def pass_on(chunk):
            send(left_all.at[chunk], left_pass_send.at[0], left_pass_recv.at[0], partner).start()

        for step in range(1, SIDE):
            for way in range(2):
                first_copy(way, step, place(way, 0)).start()
        for step in range(1, SIDE):
            for way in range(2):
                second_copy(way, 0, step, place(way, 0)).start()
        for back in (1, 3, 2):
            for way in range(2):
                chunk = place(way, back)
                first_copy(way, back, chunk).wait_recv()
                for step in range(1, SIDE):
                    second_copy(way, back, step, chunk).start()
                pass_on(chunk)
        for back in (0, 1, 3, 2):
            for way in range(2):
                three = left_all.at[pl.ds(0, SIDE - 1)]
                send(three, left_send.at[0], second_recv.at[way, back], partner).wait_recv()
                for step in range(1, SIDE):
                    pass_on(place(way, back, step))

        right_swap_1.wait_recv()
        multiply(r, first=True)

        def received(group, count):
            send(right_all.at[pl.ds(0, count)], pass_send.at[0], pass_recv.at[group], partner).wait_recv()

        begun = 0
        while begun < steps - 2:
            count = min(4, steps - 2 - begun)
            received(pass_group(begun), count)
            lax.fori_loop(begun, begun + count, lambda step, _: (multiply_step(step), None)[1], None)
            begun += count
        received(pass_group(steps - 2), 1)
        multiply_step(steps - 2)
        send(right_all.at[0, 0], pass_send.at[0], pass_recv.at[pass_group(steps - 1)], partner).wait_recv()
        multiply(origin(0, steps - 1))

    rows = acc.shape[0]
    column_sum = None
    for tall in range(2):
        parts = []
        for wide in range(2):
            span = (slice(tall * tile, (tall + 1) * tile), slice(wide * tile, (wide + 1) * tile))
            value = acc[span]
            value = value * value * prune_mask[tall, wide].astype(jnp.float32)
            acc[span] = value
            parts.append(jnp.sum(value, axis=0, keepdims=True))
        part = jnp.concatenate(parts, axis=1)
        column_sum = part if column_sum is None else column_sum + part
    own_sum[0] = column_sum

    far_first = [steps]
    for step in range(steps - 1, 0, -1):
        far_first += [step, nz - step]
    for index, step in enumerate(far_first):
        pltpu.make_async_remote_copy(
            src_ref=own_sum.at[0],
            dst_ref=sums.at[index],
            send_sem=sum_sem.at[0],
            recv_sem=sum_sem.at[1],
            device_id=at_z(step),
            device_id_type=MESH,
        ).start()

    @pl.when(l == 1)
    def _():
        right_swap_1.wait_send()
        left_swap_1.wait_send()
        send(right_all.at[pl.ds(0, nz - 1)], ring_send.at[0], ring_recv.at[0, 0, 0], partner).wait_send()
        send(right_all.at[pl.ds(0, nz - 1), 0], pass_send.at[0], pass_recv.at[0], partner).wait_send()

    @pl.when(l == 0)
    def _():
        right_swap_0.wait_send()
        send(left_all.at[pl.ds(0, nz - 2)], left_send.at[0], left_pass_recv.at[0], partner).wait_send()
        send(left_all.at[pl.ds(0, nz - 1)], left_pass_send.at[0], left_pass_recv.at[0], partner).wait_send()

    every = send(sums, sum_sem.at[0], sum_sem.at[1], partner)
    every.wait_recv()
    total = own_sum[0]
    for index in range(nz - 1):
        total += sums[index]
    out_ref[...] = acc[...] * ((rows * nz) / (total + epsilon))
    every.wait_send()


def on_device(nz, left_blocks, batch_blocks, left_mask, batch_mask, prune_mask):
    rows, _, depth = left_blocks.shape
    _, inner, columns = batch_blocks.shape
    tile = rows // left_mask.shape[0]
    half = columns // 2
    left = left_blocks.reshape(rows, depth)
    right = batch_blocks.reshape(inner, columns)
    dma = pltpu.SemaphoreType.DMA
    hbm = pl.BlockSpec(memory_space=pl.ANY)
    smem = pl.BlockSpec(memory_space=pltpu.SMEM)
    groups = (nz // 2 - 2 + 3) // 4 + 2
    return pl.pallas_call(
        functools.partial(kernel, nz),
        out_shape=pltpu.VMEM((rows, half), jnp.float32),
        in_specs=[hbm, hbm, smem, smem, smem],
        out_specs=pl.BlockSpec(memory_space=pltpu.VMEM),
        scratch_shapes=[
            pltpu.VMEM((rows, depth), jnp.bfloat16),
            pltpu.VMEM((inner, columns), jnp.bfloat16),
            pltpu.VMEM((nz, 2, rows, tile), jnp.bfloat16),
            pltpu.VMEM((nz, 2, 2 * inner, half), jnp.bfloat16),
            pltpu.VMEM((rows, half), jnp.float32),
            pltpu.VMEM((1, 1, half), jnp.float32),
            pltpu.VMEM((nz - 1, 1, half), jnp.float32),
            dma((2,)),
            dma((2,)),
            dma((2,)),
            dma((1,)),
            dma((2, 4, 4)),
            dma((1,)),
            dma((groups,)),
            dma((1,)),
            dma((2, SIDE - 1)),
            dma((2, SIDE)),
            dma((1,)),
            dma((1,)),
            dma((2,)),
        ],
        compiler_params=pltpu.CompilerParams(collective_id=0, has_side_effects=True),
    )(left, right, left_mask, batch_mask, prune_mask)


def solution(mesh):
    placed = (
        P("row", "layer", "col"),
        P("layer", "row", "col"),
        P("row", "layer", "col"),
        P("layer", "row", "col"),
        P("row", ("col", "layer")),
    )
    return jax.shard_map(
        functools.partial(on_device, mesh.shape["row"]),
        mesh=mesh,
        in_specs=placed,
        out_specs=P("row", ("col", "layer")),
        check_vma=False,
    )
```

time: 341 us -> 82.7 us (0.24)
  waiting for transfers between devices: 256 us -> 0 us
  Pallas kernels: 0 us -> 81.5 us
  blocking collectives: 58.9 us -> 0 us
  between operations: 13.1 us -> 0.01 us
  other arithmetic: 7.21 us -> 0 us
  matrix products: 4.87 us -> 0 us
    all_gather x2 -> x0, waiting for transfers between devices: 237 us -> none  [the longest x1 146 us: on_device(): complete_right = lax.all_gather(right, 'row', axis=1, tiled=True)[0]]
    pallas_call x0 -> x1, Pallas kernels: none -> 81.5 us  [on_device(): pl.pallas_call(functools.partial(kernel, nz), out_shape=pltpu.VMEM((rows,...]
    psum x1 -> x0, blocking collectives: 58.9 us -> none  [on_device(): col_sums = lax.psum(jnp.sum(inflated, axis=0), 'row')]
    reduce_scatter x1 -> x0, waiting for transfers between devices: 19.2 us -> none  [on_device(): lax.psum_scatter(product, 'layer', scatter_dimension=1, tiled=True)]
    dot_general x1 -> x0, matrix products: 4.87 us -> none  [on_device(): jnp.dot(lax.all_gather(left, 'col', axis=2, tiled=True)[:, 0, :], complet...]
    mul x3 -> x0, other arithmetic: 4.85 us -> none  [the longest x1 1.69 us: on_device(): return inflated * (total_rows / (col_sums + epsilon))]
  transfers between devices with their start and end apart: 3 -> 0, of which waited for: 3 -> 0; matrix products, arithmetic and copies ran while one was open for 1% -> 0% of each run, Pallas kernels for 0% -> 0%
where the time goes in v2:
time: 82.7 us; the launch traced here: 82.2 us
  Pallas kernels  81.5 us (99%)
    pallas_call x1, Pallas kernels, on_device(): pl.pallas_call(functools.partial(kernel, nz), out_shape=pltpu.VMEM((rows,...  81.5 us

profile of v2, /device:TPU:6, one launch (start us, length us, event | category | flops | bytes accessed | tf_op | source)
XLA Modules:
  0.0 82.2 jit_solution(17279058905642170145)
XLA Ops:
  0.0 81.5 %shard_map.55 = f32[256,256]{1,0:T(8,128)S(1)} custom-call(bf16[256,256]{1,0:T(8,128)(2,1)} %bitcast.2, bf16[128,512]{1,0:T(8,128)(2,1)} %bitcast.3, s32[2,1,2]{2,1,0:T(1,128)} %left_mask.1, s32[1,1,4]{2,1,0:T(1,128)} %right_mask.1, s32[2,2]{1,0:T(2,128)} %prune_mask.1), custom_call_target="tpu_custom_call" | custom-call | tf_op jit(solution)/shard_map/pallas_call | solution.py:308
  81.5 0.7 copy.7

commit v3 on v2

--- a/solution.py
+++ b/solution.py
@@ -10,18 +10,24 @@
 epsilon = 1e-06
 MESH = pl.DeviceIdType.MESH
 SIDE = 4
+PARTS = 2
+SLOTS = 3
+BEGIN = 9
 
 
 def kernel(
     nz,
     left_ref,
     right_ref,
+    left_mask_ref,
+    right_mask_ref,
+    prune_mask_ref,
+    out_ref,
+    left_in,
+    right_in,
     left_mask,
     right_mask,
     prune_mask,
-    out_ref,
-    left_in,
-    right_in,
     left_all,
     right_all,
     acc,
@@ -48,7 +54,6 @@
     deep = left_all.shape[3]
     tile = deep
     half = right_all.shape[3]
-    slots = ring_recv.shape[2]
 
     def at_z(step):
         return (lax.rem(r + step + nz, nz), c, l)
@@ -71,11 +76,6 @@
             device_id_type=MESH,
         )
 
-    take_right = pltpu.make_async_copy(right_ref, right_in, in_sem.at[0])
-    take_left = pltpu.make_async_copy(left_ref, left_in, in_sem.at[1])
-    take_right.start()
-    take_left.start()
-
     barrier = pltpu.get_barrier_semaphore()
 
     def greet(devices):
@@ -88,8 +88,24 @@
     pl.when(l == 1)(lambda: greet(ring_greeted))
     pl.when(l == 0)(lambda: greet(left_greeted))
 
+    fetches = [
+        pltpu.make_async_copy(source, target, in_sem.at[index])
+        for index, (source, target) in enumerate(
+            (
+                (right_ref, right_in),
+                (right_mask_ref, right_mask),
+                (left_ref, left_in),
+                (left_mask_ref, left_mask),
+                (prune_mask_ref, prune_mask),
+            )
+        )
+    ]
+    for fetch in fetches:
+        fetch.start()
+
     own_slice = pl.ds(pl.multiple_of(l * deep, deep), deep)
-    take_right.wait()
+    fetches[0].wait()
+    fetches[1].wait()
     for h in range(2):
         for part in range(half // tile):
             mask = right_mask[0, 0, h * (half // tile) + part].astype(jnp.float32)
@@ -97,14 +113,16 @@
             right_all[r, h, own_slice, part * tile : (part + 1) * tile] = (block.astype(jnp.float32) * mask).astype(
                 jnp.bfloat16
             )
-    take_left.wait()
-    for tall in range(2):
-        for wide in range(2):
-            mask = left_mask[tall, 0, wide].astype(jnp.float32)
-            block = left_in[tall * tile : (tall + 1) * tile, wide * tile : (wide + 1) * tile]
-            left_all[2 * c + wide, l, tall * tile : (tall + 1) * tile, :] = (block.astype(jnp.float32) * mask).astype(
-                jnp.bfloat16
-            )
+    def mask_left():
+        fetches[2].wait()
+        fetches[3].wait()
+        for tall in range(2):
+            for wide in range(2):
+                mask = left_mask[tall, 0, wide].astype(jnp.float32)
+                block = left_in[tall * tile : (tall + 1) * tile, wide * tile : (wide + 1) * tile]
+                left_all[2 * c + wide, l, tall * tile : (tall + 1) * tile, :] = (
+                    block.astype(jnp.float32) * mask
+                ).astype(jnp.bfloat16)
 
     ways = (1, -1)
 
@@ -114,7 +132,10 @@
     def multiply(row, first=False):
         left = jnp.concatenate([left_all[row, 0], left_all[row, 1]], axis=1)
         product = jnp.dot(left, right_all[row, l], preferred_element_type=jnp.float32)
-        acc[...] = product if first else acc[...] + product
+        if first:
+            acc[...] = product
+        else:
+            acc[...] += product
 
     def multiply_step(step):
         for way in range(2):
@@ -134,32 +155,40 @@
     @pl.when(l == 1)
     def _():
         pl.semaphore_wait(barrier, 1 + len(ring_greeted))
-        kinds = ((1, 0), (1, 1), (0, 0), (0, 1))
+        kinds = tuple((s, h, part) for s in (1, 0) for h in (0, 1) for part in range(PARTS))
         hops = ((steps - 1, steps), (steps, steps - 1))
 
         def block(kind, row):
-            s, h = kinds[kind]
-            return right_all.at[row, h, pl.ds(s * deep, deep)]
+            s, h, part = kinds[kind]
+            return right_all.at[row, h, pl.ds(s * deep + part * (deep // PARTS), deep // PARTS)]
 
         def ring_copy(way, kind, step, row):
-            return send(
-                block(kind, row), ring_send.at[0], ring_recv.at[way, kind, lax.rem(step, slots)], at_z(ways[way])
-            )
-
-        for kind in range(2):
+            s, h, _ = kinds[kind]
+            recv_sem, device = ring_recv.at[way, kind, lax.rem(step, SLOTS)], at_z(ways[way])
+            if isinstance(step, int) and final(way, kind, step):
+                recv_sem, device = pass_recv.at[pass_group(step)], (device[0], c, 0)
+            return send(block(kind, row), ring_send.at[0], recv_sem, device)
+
+        def final(way, kind, step):
+            s, h, _ = kinds[kind]
+            return h == 0 and step == hops[s][way] - 1
+
+        for kind in range(2 * PARTS):
             for way in range(2):
                 ring_copy(way, kind, 0, r).start()
         right_swap_1.start()
+        mask_left()
         left_swap_1.start()
         right_swap_0.wait_recv()
-        for kind in range(2, 4):
+        for kind in range(2 * PARTS, 4 * PARTS):
             for way in range(2):
                 ring_copy(way, kind, 0, r).start()
 
-        def ring_step(step, last=False):
-            for kind, (s, h) in enumerate(kinds):
+        def ring_step(step):
+            last = isinstance(step, int)
+            for kind, (s, h, _) in enumerate(kinds):
                 for way in range(2):
-                    if last and step >= hops[s][way]:
+                    if last and (step >= hops[s][way] or final(way, kind, step)):
                         continue
                     row = origin(way, step)
                     ring_copy(way, kind, step, row).wait_recv()
@@ -168,9 +197,9 @@
                     if h == 0:
                         send(block(kind, row), pass_send.at[0], pass_recv.at[pass_group(step)], partner).start()
 
-        begin = steps - 6
-        end = steps - 2
-        each = begin // (end - begin) + 1
+        begin = BEGIN
+        end = steps - 3
+        each = -(-(steps - 1) // (steps - 1 - begin))
         lax.fori_loop(0, begin, lambda step, _: (ring_step(step), None)[1], None)
         send(left_all.at[pl.ds(0, nz - 1)], left_pass_send.at[0], left_pass_recv.at[0], partner).wait_recv()
         multiply(r, first=True)
@@ -181,16 +210,20 @@
                 multiply_step(each * (step - begin) + turn)
 
         lax.fori_loop(begin, end, both, None)
-        ring_step(end, last=True)
-        for step in range(each * (end - begin), end + 1):
-            multiply_step(step)
-        ring_step(end + 1, last=True)
-        multiply(origin(0, end + 1))
+        done = each * (end - begin)
+        for step in range(end, steps - 1):
+            ring_step(step)
+            until = min(done + each, step + 1) if step < steps - 2 else step + 1
+            for turn in range(done, until):
+                multiply_step(turn)
+            done = until
+        ring_step(steps - 1)
 
     @pl.when(l == 0)
     def _():
         pl.semaphore_wait(barrier, 1 + len(left_greeted))
         right_swap_0.start()
+        mask_left()
         left_swap_0.start()
         left_swap_1.wait_recv()
         peers = (at_x, at_y)
@@ -243,16 +276,18 @@
         received(pass_group(steps - 2), 1)
         multiply_step(steps - 2)
         send(right_all.at[0, 0], pass_send.at[0], pass_recv.at[pass_group(steps - 1)], partner).wait_recv()
-        multiply(origin(0, steps - 1))
-
+
+    fetches[4].wait()
     rows = acc.shape[0]
     column_sum = None
+    row = origin(0, steps - 1)
+    left = jnp.concatenate([left_all[row, 0], left_all[row, 1]], axis=1)
+    product = acc[...] + jnp.dot(left, right_all[row, l], preferred_element_type=jnp.float32)
     for tall in range(2):
         parts = []
         for wide in range(2):
             span = (slice(tall * tile, (tall + 1) * tile), slice(wide * tile, (wide + 1) * tile))
-            value = acc[span]
-            value = value * value * prune_mask[tall, wide].astype(jnp.float32)
+            value = product[span] * product[span] * prune_mask[tall, wide].astype(jnp.float32)
             acc[span] = value
             parts.append(jnp.sum(value, axis=0, keepdims=True))
         part = jnp.concatenate(parts, axis=1)
@@ -277,7 +312,7 @@
         right_swap_1.wait_send()
         left_swap_1.wait_send()
         send(right_all.at[pl.ds(0, nz - 1)], ring_send.at[0], ring_recv.at[0, 0, 0], partner).wait_send()
-        send(right_all.at[pl.ds(0, nz - 1), 0], pass_send.at[0], pass_recv.at[0], partner).wait_send()
+        send(right_all.at[pl.ds(0, nz - 3), 0], pass_send.at[0], pass_recv.at[0], partner).wait_send()
 
     @pl.when(l == 0)
     def _():
@@ -303,26 +338,28 @@
     right = batch_blocks.reshape(inner, columns)
     dma = pltpu.SemaphoreType.DMA
     hbm = pl.BlockSpec(memory_space=pl.ANY)
-    smem = pl.BlockSpec(memory_space=pltpu.SMEM)
     groups = (nz // 2 - 2 + 3) // 4 + 2
     return pl.pallas_call(
         functools.partial(kernel, nz),
         out_shape=pltpu.VMEM((rows, half), jnp.float32),
-        in_specs=[hbm, hbm, smem, smem, smem],
+        in_specs=[hbm] * 5,
         out_specs=pl.BlockSpec(memory_space=pltpu.VMEM),
         scratch_shapes=[
             pltpu.VMEM((rows, depth), jnp.bfloat16),
             pltpu.VMEM((inner, columns), jnp.bfloat16),
+            pltpu.SMEM(left_mask.shape, jnp.int32),
+            pltpu.SMEM(batch_mask.shape, jnp.int32),
+            pltpu.SMEM(prune_mask.shape, jnp.int32),
             pltpu.VMEM((nz, 2, rows, tile), jnp.bfloat16),
             pltpu.VMEM((nz, 2, 2 * inner, half), jnp.bfloat16),
             pltpu.VMEM((rows, half), jnp.float32),
             pltpu.VMEM((1, 1, half), jnp.float32),
             pltpu.VMEM((nz - 1, 1, half), jnp.float32),
+            dma((5,)),
             dma((2,)),
             dma((2,)),
-            dma((2,)),
-            dma((1,)),
-            dma((2, 4, 4)),
+            dma((1,)),
+            dma((2, 4 * PARTS, SLOTS)),
             dma((1,)),
             dma((groups,)),
             dma((1,)),

time: 82.7 us -> 81.2 us (0.982)
  Pallas kernels: 81.5 us -> 79.3 us
    pallas_call x1, Pallas kernels: 81.5 us -> 79.3 us  [on_device(): pl.pallas_call(functools.partial(kernel, nz), out_shape=pltpu.VMEM((rows,...]
where the time goes in v3:
time: 81.2 us; the launch traced here: 80 us
  Pallas kernels  79.3 us (98%)
    pallas_call x1, Pallas kernels, on_device(): pl.pallas_call(functools.partial(kernel, nz), out_shape=pltpu.VMEM((rows,...  79.3 us

profile of v3, /device:TPU:6, one launch (start us, length us, event | category | flops | bytes accessed | tf_op | source)
XLA Modules:
  0.0 80.0 jit_solution(2817091233841216919)
XLA Ops:
  0.0 79.3 %shard_map.55 = f32[256,256]{1,0:T(8,128)S(1)} custom-call(bf16[256,256]{1,0:T(8,128)(2,1)} %bitcast.2, bf16[128,512]{1,0:T(8,128)(2,1)} %bitcast.3, s32[2,1,2]{2,1,0:T(1,128)} %left_mask_ref.1, s32[1,1,4]{2,1,0:T(1,128)} %right_mask_ref.1, s32[2,2]{1,0:T(2,128)} %prune_mask_ref.1), custom_call_target="tpu_custom_call" | custom-call | tf_op jit(solution)/shard_map/pallas_call | solution.py:342
  79.3 0.7 copy.7

commit v4 on v3

--- a/solution.py
+++ b/solution.py
@@ -59,10 +59,10 @@
         return (lax.rem(r + step + nz, nz), c, l)
 
     def at_x(step):
-        return (r, y * SIDE + lax.rem(x + step, SIDE), l)
+        return (r, y * SIDE + lax.rem(x + step + SIDE, SIDE), l)
 
     def at_y(step):
-        return (r, lax.rem(y + step, SIDE) * SIDE + x, l)
+        return (r, lax.rem(y + step + SIDE, SIDE) * SIDE + x, l)
 
     partner = (r, c, 1 - l)
 
@@ -82,11 +82,9 @@
         for device in devices:
             pl.semaphore_signal(barrier, inc=1, device_id=device, device_id_type=MESH)
 
-    greet([partner])
-    ring_greeted = [at_z(1), at_z(-1)]
-    left_greeted = [peer(step) for step in range(1, SIDE) for peer in (at_x, at_y)]
-    pl.when(l == 1)(lambda: greet(ring_greeted))
-    pl.when(l == 0)(lambda: greet(left_greeted))
+    heard = (2, 7)
+    pl.when(l == 1)(lambda: greet([at_z(1), at_z(-1), (at_z(1)[0], c, 0), (at_z(-1)[0], c, 0), partner]))
+    pl.when(l == 0)(lambda: greet([at_x(1), at_x(-1), at_y(1), at_y(-1)]))
 
     fetches = [
         pltpu.make_async_copy(source, target, in_sem.at[index])
@@ -113,6 +111,7 @@
             right_all[r, h, own_slice, part * tile : (part + 1) * tile] = (block.astype(jnp.float32) * mask).astype(
                 jnp.bfloat16
             )
+
     def mask_left():
         fetches[2].wait()
         fetches[3].wait()
@@ -152,37 +151,36 @@
             return (steps - 2 + 3) // 4 + step - (steps - 2)
         return step // 4
 
+    kinds = tuple((s, h, part) for s in (1, 0) for h in (0, 1) for part in range(PARTS))
+    hops = ((steps - 1, steps), (steps, steps - 1))
+
+    def block(kind, row):
+        s, h, part = kinds[kind]
+        return right_all.at[row, h, pl.ds(s * deep + part * (deep // PARTS), deep // PARTS)]
+
+    def ring_copy(way, kind, step, row, core=None):
+        s, h, _ = kinds[kind]
+        recv_sem, device = ring_recv.at[way, kind, lax.rem(step, SLOTS)], at_z(ways[way])
+        if core is not None:
+            device = (device[0], c, core)
+        if isinstance(step, int) and final(way, kind, step):
+            recv_sem, device = pass_recv.at[pass_group(step)], (device[0], c, 0)
+        return send(block(kind, row), ring_send.at[0], recv_sem, device)
+
+    def final(way, kind, step):
+        s, h, _ = kinds[kind]
+        return h == 0 and step == hops[s][way] - 1
+
     @pl.when(l == 1)
     def _():
-        pl.semaphore_wait(barrier, 1 + len(ring_greeted))
-        kinds = tuple((s, h, part) for s in (1, 0) for h in (0, 1) for part in range(PARTS))
-        hops = ((steps - 1, steps), (steps, steps - 1))
-
-        def block(kind, row):
-            s, h, part = kinds[kind]
-            return right_all.at[row, h, pl.ds(s * deep + part * (deep // PARTS), deep // PARTS)]
-
-        def ring_copy(way, kind, step, row):
-            s, h, _ = kinds[kind]
-            recv_sem, device = ring_recv.at[way, kind, lax.rem(step, SLOTS)], at_z(ways[way])
-            if isinstance(step, int) and final(way, kind, step):
-                recv_sem, device = pass_recv.at[pass_group(step)], (device[0], c, 0)
-            return send(block(kind, row), ring_send.at[0], recv_sem, device)
-
-        def final(way, kind, step):
-            s, h, _ = kinds[kind]
-            return h == 0 and step == hops[s][way] - 1
-
+        pl.semaphore_wait(barrier, heard[0])
         for kind in range(2 * PARTS):
             for way in range(2):
                 ring_copy(way, kind, 0, r).start()
+        mask_left()
+        right_swap_0.wait_recv()
         right_swap_1.start()
-        mask_left()
         left_swap_1.start()
-        right_swap_0.wait_recv()
-        for kind in range(2 * PARTS, 4 * PARTS):
-            for way in range(2):
-                ring_copy(way, kind, 0, r).start()
 
         def ring_step(step):
             last = isinstance(step, int)
@@ -221,7 +219,10 @@
 
     @pl.when(l == 0)
     def _():
-        pl.semaphore_wait(barrier, 1 + len(left_greeted))
+        pl.semaphore_wait(barrier, heard[1])
+        for kind in range(2 * PARTS, 4 * PARTS):
+            for way in range(2):
+                ring_copy(way, kind, 0, r, core=1).start()
         right_swap_0.start()
         mask_left()
         left_swap_0.start()
@@ -241,16 +242,22 @@
         def pass_on(chunk):
             send(left_all.at[chunk], left_pass_send.at[0], left_pass_recv.at[0], partner).start()
 
-        for step in range(1, SIDE):
-            for way in range(2):
-                first_copy(way, step, place(way, 0)).start()
-        for step in range(1, SIDE):
-            for way in range(2):
-                second_copy(way, 0, step, place(way, 0)).start()
+        near = (1, SIDE - 1)
+        for copy in (first_copy, functools.partial(second_copy, back=0)):
+            for step in near:
+                for way in range(2):
+                    copy(way, step=step, chunk=place(way, 0)).start()
+        for way in range(2):
+            first_copy(way, 1, place(way, 1)).wait_recv()
+        for copy in (first_copy, functools.partial(second_copy, back=0)):
+            for step in range(2, SIDE - 1):
+                for way in range(2):
+                    copy(way, step=step, chunk=place(way, 0)).start()
         for back in (1, 3, 2):
             for way in range(2):
                 chunk = place(way, back)
-                first_copy(way, back, chunk).wait_recv()
+                if back != 1:
+                    first_copy(way, back, chunk).wait_recv()
                 for step in range(1, SIDE):
                     second_copy(way, back, step, chunk).start()
                 pass_on(chunk)
@@ -311,12 +318,13 @@
     def _():
         right_swap_1.wait_send()
         left_swap_1.wait_send()
-        send(right_all.at[pl.ds(0, nz - 1)], ring_send.at[0], ring_recv.at[0, 0, 0], partner).wait_send()
+        send(right_all.at[pl.ds(0, nz - 2)], ring_send.at[0], ring_recv.at[0, 0, 0], partner).wait_send()
         send(right_all.at[pl.ds(0, nz - 3), 0], pass_send.at[0], pass_recv.at[0], partner).wait_send()
 
     @pl.when(l == 0)
     def _():
         right_swap_0.wait_send()
+        send(right_all.at[0], ring_send.at[0], ring_recv.at[0, 0, 0], partner).wait_send()
         send(left_all.at[pl.ds(0, nz - 2)], left_send.at[0], left_pass_recv.at[0], partner).wait_send()
         send(left_all.at[pl.ds(0, nz - 1)], left_pass_send.at[0], left_pass_recv.at[0], partner).wait_send()
 

time: 81.2 us -> 80.8 us (level)
  no operation moved by 1% of the time
where the time goes in v4:
time: 80.8 us; the launch traced here: 79.9 us
  Pallas kernels  79.2 us (98%)
    pallas_call x1, Pallas kernels, on_device(): pl.pallas_call(functools.partial(kernel, nz), out_shape=pltpu.VMEM((rows,...  79.2 us

profile of v4, /device:TPU:6, one launch (start us, length us, event | category | flops | bytes accessed | tf_op | source)
XLA Modules:
  0.0 79.9 jit_solution(4418846299110555538)
XLA Ops:
  0.0 79.2 %shard_map.55 = f32[256,256]{1,0:T(8,128)S(1)} custom-call(bf16[256,256]{1,0:T(8,128)(2,1)} %bitcast.2, bf16[128,512]{1,0:T(8,128)(2,1)} %bitcast.3, s32[2,1,2]{2,1,0:T(1,128)} %left_mask_ref.1, s32[1,1,4]{2,1,0:T(1,128)} %right_mask_ref.1, s32[2,2]{1,0:T(2,128)} %prune_mask_ref.1), custom_call_target="tpu_custom_call" | custom-call | tf_op jit(solution)/shard_map/pallas_call | solution.py:350
  79.2 0.7 copy.7

commit v5 on v4

--- a/solution.py
+++ b/solution.py
@@ -12,7 +12,7 @@
 SIDE = 4
 PARTS = 2
 SLOTS = 3
-BEGIN = 9
+BEGIN = 10
 
 
 def kernel(

time: 80.8 us -> 80.7 us (level)
  no operation moved by 1% of the time
where the time goes in v5:
time: 80.7 us; the launch traced here: 79.6 us
  Pallas kernels  78.9 us (98%)
    pallas_call x1, Pallas kernels, on_device(): pl.pallas_call(functools.partial(kernel, nz), out_shape=pltpu.VMEM((rows,...  78.9 us

profile of v5, /device:TPU:6, one launch (start us, length us, event | category | flops | bytes accessed | tf_op | source)
XLA Modules:
  0.0 79.6 jit_solution(12521323757472598135)
XLA Ops:
  0.0 78.9 %shard_map.55 = f32[256,256]{1,0:T(8,128)S(1)} custom-call(bf16[256,256]{1,0:T(8,128)(2,1)} %bitcast.2, bf16[128,512]{1,0:T(8,128)(2,1)} %bitcast.3, s32[2,1,2]{2,1,0:T(1,128)} %left_mask_ref.1, s32[1,1,4]{2,1,0:T(1,128)} %right_mask_ref.1, s32[2,2]{1,0:T(2,128)} %prune_mask_ref.1), custom_call_target="tpu_custom_call" | custom-call | tf_op jit(solution)/shard_map/pallas_call | solution.py:350
  78.9 0.7 copy.7
